TPU v7x, 512 devices: a whole 4x4x16 slice. The times are simulated.
512 devices in a mesh: rows: 8 (over x_lo, y), cols: 64 (over z, x_hi, core).
Axes of the slice: x: 4 (x_hi: 2, x_lo: 2; x = x_hi * 2 + x_lo), y: 4, z: 16, core: 2. Of those that a mesh axis runs over, the one named last changes fastest.
Arguments:
- points: bfloat16 [32, 16384], P(None, ('rows', 'cols')), may hold values from 0 to 1
- samples: bfloat16 [32, 32768], P(None, 'cols'), may hold values from -0.5 to 1.5
- potential: float32 [32768], P('cols'), may hold values from -6 to 60
Outputs:
- point_potential: float32 [16384], P(('rows', 'cols'))
- sample_potential: float32 [32768], P('cols')
- barycenter: float32 [32, 16384], P(None, ('rows', 'cols'))
All inputs are finite; a program needn't handle non-finite values.
Results may differ from a plain program's by a relative error of at most 0.00055.
Values may be sent and summed in bfloat16 or wider, within the bound.
No kernel may reach another device: no remote copies, remote signals or barrier semaphores. Data moves between devices by JAX's collectives and lax.ppermute only.
A program may use at most 64 MiB of HBM per device.

v0:
```python
import math
import jax
import jax.numpy as jnp
from jax import lax
from jax.sharding import PartitionSpec as P

EPS = 0.25


def joined(part, axis, combine):
    gathered = jax.tree.map(lambda a: lax.all_gather(a, axis), part)

    def take(source):
        return jax.tree.map(lambda a: lax.dynamic_index_in_dim(a, source, 0, False), gathered)

    return lax.fori_loop(
        1, lax.axis_size(axis), lambda source, state: combine(state, take(source)), take(0)
    )


def combine_stats(first, second):
    top = jnp.maximum(first[0], second[0])
    total = first[1] * jnp.exp(first[0] - top) + second[1] * jnp.exp(second[0] - top)
    return (top, total)


def on_device(points, samples, potential):
    own_count = points.shape[1]
    whole = lax.all_gather(points, "cols", axis=1, tiled=True)
    block_count = whole.shape[1]
    col_count = lax.axis_size("cols")
    total_samples = samples.shape[1] * col_count
    total_points = block_count * lax.axis_size("rows")
    xf = whole.astype(jnp.float32)
    yf = samples.astype(jnp.float32)
    point_sq = jnp.sum(xf * xf, axis=0)
    sample_sq = jnp.sum(yf * yf, axis=0)
    cross = lax.dot_general(
        whole, samples, (((0,), (0,)), ((), ())), preferred_element_type=jnp.float32
    )
    cost = 0.5 * point_sq[:, None] + 0.5 * sample_sq[None, :] - cross
    score = (potential[None, :] - cost) / EPS
    row_top = lax.pmax(jnp.max(score, axis=1), "cols")
    row_sum = lax.psum(jnp.sum(jnp.exp(score - row_top[:, None]), axis=1), "cols")
    point_full = -EPS * (row_top + jnp.log(row_sum) - math.log(total_samples))
    col_score = (point_full[:, None] - cost) / EPS
    col_top = jnp.max(col_score, axis=0)
    col_sum = jnp.sum(jnp.exp(col_score - col_top[None, :]), axis=0)
    col_top, col_sum = joined((col_top, col_sum), "rows", combine_stats)
    sample_potential = -EPS * (col_top + jnp.log(col_sum) - math.log(total_points))
    new_score = (sample_potential[None, :] - cost) / EPS
    block_top = jnp.max(new_score, axis=1)
    weight = jnp.exp(new_score - block_top[:, None]).astype(jnp.bfloat16)
    denom = jnp.sum(weight.astype(jnp.float32), axis=1)
    numer = lax.dot_general(
        samples, weight, (((1,), (1,)), ((), ())), preferred_element_type=jnp.float32
    )
    position = lax.axis_index("cols") * own_count
    new_top = lax.pmax(block_top, "cols")
    scale = jnp.exp(block_top - new_top)
    numer_scaled = numer * scale[None, :]
    denom_scaled = denom * scale
    numer_all, denom_all = lax.psum((numer_scaled, denom_scaled), "cols")
    numer_own = lax.dynamic_slice_in_dim(numer_all, position, own_count, 1)
    denom_own = lax.dynamic_slice_in_dim(denom_all, position, own_count, 0)
    barycenter = numer_own / denom_own[None, :]
    point_potential = lax.dynamic_slice_in_dim(point_full, position, own_count, 0)
    return (point_potential, sample_potential, barycenter)


def solution(mesh):
    placed = (P(None, ("rows", "cols")), P(None, "cols"), P("cols"))
    return jax.shard_map(
        on_device,
        mesh=mesh,
        in_specs=placed,
        out_specs=(P(("rows", "cols")), P("cols"), P(None, ("rows", "cols"))),
        check_vma=False,
    )
```

profile of v0, /device:TPU:1, one launch (start us, length us, event | category | flops | bytes accessed | tf_op | source)
XLA Modules:
  0.0 1036.2 jit_solution(15728335356451031905)
XLA Ops:
  7.2 0.0 copy-start.4
  7.2 0.0 all-reduce.2.cloned.1.call-start
  7.2 0.8 multiply_reduce_fusion.1
  8.0 0.8 copy.6
  8.8 86.0 %all_gather.15 = bf16[32,2048]{0,1:T(8,128)(2,1)S(1)} all-gather(bf16[32,32]{0,1:T(8,128)(2,1)S(1)} %copy.6), channel_id=1, replica_groups=mesh['rows'=8,'cols'=64] {'cols'}, dimensions={1}, use_global_device_ids=true | all-gather | bytes 133120 | tf_op jit(solution)/shard_map/all_gather | solution.py:29
  94.8 0.3 multiply_reduce_fusion
  95.2 3.6 fusion
  98.8 130.3 %pmax.14 = f32[2048]{0:T(1024)S(1)} all-reduce(f32[2048]{0:T(1024)S(1)} %get-tuple-element.156), channel_id=1, replica_groups=mesh['rows'=8,'cols'=64] {'cols'}, use_global_device_ids=true, to_apply=%region_3.0 | all-reduce | flops 2048 | bytes 16384 | tf_op jit(solution)/shard_map/pmax | solution.py:43
  229.1 0.0 copy-done.4
  229.1 3.1 exponential_reduce_fusion.1
  232.2 131.1 %psum.21 = f32[2048]{0:T(1024)S(1)} all-reduce(f32[2048]{0:T(1024)S(1)} %exponential_reduce_fusion.1), channel_id=1, replica_groups=mesh['rows'=8,'cols'=64] {'cols'}, use_global_device_ids=true, to_apply=%region_5.0 | all-reduce | flops 2048 | bytes 16384 | tf_op jit(solution)/shard_map/psum | solution.py:44
  363.4 0.0 copy-start
  363.4 2.8 fusion.1
  366.2 0.6 copy-done
  366.8 0.9 exponential_reduce_fusion
  367.7 19.0 %all-gather.2 = f32[8,1,512]{2,1,0:T(1,128)S(1)} all-gather(f32[1,1,512]{2,1,0:T(1,128)S(1)} %bitcast.28), channel_id=2, replica_groups=mesh['rows'=8,'cols'=64] {'rows'}, dimensions={0}, use_global_device_ids=true | all-gather | bytes 18432 | tf_op jit(solution)/shard_map/all_gather | solution.py:11
  386.8 19.0 %all-gather.3 = f32[8,1,512]{2,1,0:T(1,128)S(1)} all-gather(f32[1,1,512]{2,1,0:T(1,128)S(1)} %bitcast.29), channel_id=3, replica_groups=mesh['rows'=8,'cols'=64] {'rows'}, dimensions={0}, use_global_device_ids=true | all-gather | bytes 18432 | tf_op jit(solution)/shard_map/all_gather | solution.py:11
  405.8 0.4 while.17
  406.2 0.0 copy-start.1
  406.2 0.0 copy-start.3
  406.3 2.8 fusion.2
  409.1 0.6 copy-done.1
  409.7 0.0 copy-start.2
  409.7 1.1 convert_reduce_fusion
  410.8 0.0 copy-done.3
  410.8 140.0 %pmax.15 = f32[2048]{0:T(1024)S(1)} all-reduce(f32[2048]{0:T(1024)S(1)} %fusion.2), channel_id=1, replica_groups=mesh['rows'=8,'cols'=64] {'cols'}, use_global_device_ids=true, to_apply=%region_11.12 | all-reduce | flops 2048 | bytes 16384 | tf_op jit(solution)/shard_map/pmax | solution.py:59
  550.8 0.0 copy-done.2
  550.8 1.2 fusion.3
  552.0 0.0 all-reduce.2.cloned.1.call-update
  552.0 0.6 dynamic_slice.36
  552.6 130.8 %psum.23 = f32[2048]{0:T(1024)S(1)} all-reduce(f32[2048]{0:T(1024)S(1)} %get-tuple-element.150), channel_id=1, replica_groups=mesh['rows'=8,'cols'=64] {'cols'}, use_global_device_ids=true, to_apply=%region_14.15 | all-reduce | flops 2048 | bytes 16384 | tf_op jit(solution)/shard_map/psum | solution.py:63
  683.4 0.1 dynamic_slice.40
  683.5 344.5 %all-reduce.2.cloned.1.call-done = f32[32,2048]{1,0:T(8,128)} async-done(((f32[32,2048]{1,0:T(8,128)}), f32[32,2048]{1,0:T(8,128)}) %all-reduce.2.cloned.1.call-update) | async-done | bytes 262160 | tf_op jit(solution)/shard_map/psum | solution.py:63
  1028.0 1.4 dynamic-slice_divide_fusion
  (23 shorter events, 0.3 us)
Async XLA Ops:
  7.2 221.9 %copy-start.4 = (f32[512]{0:T(512)S(1)}, f32[512]{0:T(512)}, u32[]{:S(2)}) copy-start(f32[512]{0:T(512)} %param.7) | copy-start | bytes 6148
  7.2 1020.8 %all-reduce.2.cloned.1.call-start = ((), (), s32[]{:S(2)}) async-start(), calls=%async_computation | async-start | bytes 524288 | tf_op jit(solution)/shard_map/psum | solution.py:63
  363.4 3.5 copy-start
  406.2 3.5 copy-start.1
  406.2 4.5 copy-start.3
  409.7 141.1 %copy-start.2 = (bf16[32,512]{1,0:T(8,128)(2,1)S(1)}, bf16[32,512]{1,0:T(8,128)(2,1)}, u32[]{:S(2)}) copy-start(bf16[32,512]{1,0:T(8,128)(2,1)} %param.6) | copy-start | bytes 98308
Sparse Core Ops, SparseCore 0:
  552.1 475.8 all-reduce.1
where the time goes:
time: 1040 us
  blocking collectives  656 us (63%)
  waiting for transfers between devices  345 us (33%)
  between operations  14.2 us (1%)
  other arithmetic  13.5 us (1%)
    psum x1, waiting for transfers between devices, on_device(): numer_all, denom_all = lax.psum((numer_scaled, denom_scaled), 'cols')  344 us
    pmax x1, blocking collectives, on_device(): new_top = lax.pmax(block_top, 'cols')  140 us
    psum x1, blocking collectives, on_device(): lax.psum(jnp.sum(jnp.exp(score - row_top[:, None]), axis=1), 'cols')  131 us
    psum x1, blocking collectives, on_device(): numer_all, denom_all = lax.psum((numer_scaled, denom_scaled), 'cols')  131 us
    pmax x1, blocking collectives, on_device(): row_top = lax.pmax(jnp.max(score, axis=1), 'cols')  130 us
    all_gather x1, blocking collectives, on_device(): whole = lax.all_gather(points, 'cols', axis=1, tiled=True)  86 us
    all_gather x2, blocking collectives, joined(): gathered = jax.tree.map(lambda a: lax.all_gather(a, axis), part)  38.1 us
  transfers between devices with their start and end apart: 1, of which 1 were waited for; matrix products, arithmetic and copies ran while one was open for 0% of the time, Pallas kernels for 0%

commit v1 on v0

--- a/solution.py
+++ b/solution.py
@@ -41,7 +41,7 @@
     cost = 0.5 * point_sq[:, None] + 0.5 * sample_sq[None, :] - cross
     score = (potential[None, :] - cost) / EPS
     row_top = lax.pmax(jnp.max(score, axis=1), "cols")
-    row_sum = lax.psum(jnp.sum(jnp.exp(score - row_top[:, None]), axis=1), "cols")
+    row_sum = lax.all_gather(jnp.sum(jnp.exp(score - row_top[:, None]), axis=1), "cols").sum(axis=0)
     point_full = -EPS * (row_top + jnp.log(row_sum) - math.log(total_samples))
     col_score = (point_full[:, None] - cost) / EPS
     col_top = jnp.max(col_score, axis=0)

time: 1040 us -> 979 us (0.941)
  blocking collectives: 656 us -> 598 us
    psum x1 -> x0, blocking collectives: 131 us -> none  [on_device(): lax.psum(jnp.sum(jnp.exp(score - row_top[:, None]), axis=1), 'cols')]
    all_gather x0 -> x1, blocking collectives: none -> 73.6 us  [on_device(): lax.all_gather(jnp.sum(jnp.exp(score - row_top[:, None]), axis=1), 'cols')]
where the time goes in v1:
time: 979 us; the launch traced here: 978 us
  blocking collectives  598 us (61%)
  waiting for transfers between devices  345 us (35%)
  between operations  14.2 us (1%)
  other arithmetic  13.5 us (1%)
    psum x1, waiting for transfers between devices, on_device(): numer_all, denom_all = lax.psum((numer_scaled, denom_scaled), 'cols')  345 us
    pmax x1, blocking collectives, on_device(): new_top = lax.pmax(block_top, 'cols')  140 us
    psum x1, blocking collectives, on_device(): numer_all, denom_all = lax.psum((numer_scaled, denom_scaled), 'cols')  131 us
    pmax x1, blocking collectives, on_device(): row_top = lax.pmax(jnp.max(score, axis=1), 'cols')  130 us
    all_gather x1, blocking collectives, on_device(): whole = lax.all_gather(points, 'cols', axis=1, tiled=True)  86 us
    all_gather x1, blocking collectives, on_device(): lax.all_gather(jnp.sum(jnp.exp(score - row_top[:, None]), axis=1), 'cols')  73.6 us
    all_gather x2, blocking collectives, joined(): gathered = jax.tree.map(lambda a: lax.all_gather(a, axis), part)  38.1 us
  transfers between devices with their start and end apart: 1, of which 1 were waited for; matrix products, arithmetic and copies ran while one was open for 0% of the time, Pallas kernels for 0%

profile of v1, /device:TPU:1, one launch (start us, length us, event | category | flops | bytes accessed | tf_op | source)
XLA Modules:
  0.0 978.3 jit_solution(7390617975656938329)
XLA Ops:
  7.2 0.0 copy-start.4
  7.2 0.0 all-reduce.2.cloned.1.call-start
  7.2 0.8 multiply_reduce_fusion.1
  8.0 0.8 copy.7
  8.8 86.0 %all_gather.21 = bf16[32,2048]{0,1:T(8,128)(2,1)S(1)} all-gather(bf16[32,32]{0,1:T(8,128)(2,1)S(1)} %copy.7), channel_id=1, replica_groups=mesh['rows'=8,'cols'=64] {'cols'}, dimensions={1}, use_global_device_ids=true | all-gather | bytes 133120 | tf_op jit(solution)/shard_map/all_gather | solution.py:29
  94.8 0.3 multiply_reduce_fusion
  95.2 3.6 fusion
  98.8 130.3 %pmax.14 = f32[2048]{0:T(1024)S(1)} all-reduce(f32[2048]{0:T(1024)S(1)} %get-tuple-element.156), channel_id=1, replica_groups=mesh['rows'=8,'cols'=64] {'cols'}, use_global_device_ids=true, to_apply=%region_3.0 | all-reduce | flops 2048 | bytes 16384 | tf_op jit(solution)/shard_map/pmax | solution.py:43
  229.1 0.0 copy-done.4
  229.1 3.1 exponential_reduce_fusion.1
  232.2 73.6 %all-gather = f32[131072]{0:T(1024)S(1)} all-gather(f32[2048]{0:T(1024)S(1)} %exponential_reduce_fusion.1), channel_id=2, replica_groups=mesh['rows'=8,'cols'=64] {'cols'}, dimensions={0}, use_global_device_ids=true | all-gather | bytes 532480 | tf_op jit(solution)/shard_map/all_gather | solution.py:44
  305.8 0.1 reshape.22
  305.9 0.0 copy-start
  306.0 2.8 fusion.1
  308.8 0.6 copy-done
  309.4 0.9 exponential_reduce_fusion
  310.3 19.0 %all-gather.3 = f32[8,1,512]{2,1,0:T(1,128)S(1)} all-gather(f32[1,1,512]{2,1,0:T(1,128)S(1)} %bitcast.28), channel_id=3, replica_groups=mesh['rows'=8,'cols'=64] {'rows'}, dimensions={0}, use_global_device_ids=true | all-gather | bytes 18432 | tf_op jit(solution)/shard_map/all_gather | solution.py:11
  329.4 19.0 %all-gather.4 = f32[8,1,512]{2,1,0:T(1,128)S(1)} all-gather(f32[1,1,512]{2,1,0:T(1,128)S(1)} %bitcast.29), channel_id=4, replica_groups=mesh['rows'=8,'cols'=64] {'rows'}, dimensions={0}, use_global_device_ids=true | all-gather | bytes 18432 | tf_op jit(solution)/shard_map/all_gather | solution.py:11
  348.4 0.4 while.17
  348.8 0.0 copy-start.1
  348.8 0.0 copy-start.3
  348.8 2.8 fusion.2
  351.7 0.6 copy-done.1
  352.2 0.0 copy-start.2
  352.2 1.1 convert_reduce_fusion
  353.3 0.0 copy-done.3
  353.3 139.6 %pmax.15 = f32[2048]{0:T(1024)S(1)} all-reduce(f32[2048]{0:T(1024)S(1)} %fusion.2), channel_id=1, replica_groups=mesh['rows'=8,'cols'=64] {'cols'}, use_global_device_ids=true, to_apply=%region_11.12 | all-reduce | flops 2048 | bytes 16384 | tf_op jit(solution)/shard_map/pmax | solution.py:59
  492.9 0.0 copy-done.2
  492.9 1.2 fusion.3
  494.1 0.0 all-reduce.2.cloned.1.call-update
  494.1 0.6 dynamic_slice.36
  494.7 130.7 %psum.15 = f32[2048]{0:T(1024)S(1)} all-reduce(f32[2048]{0:T(1024)S(1)} %get-tuple-element.150), channel_id=1, replica_groups=mesh['rows'=8,'cols'=64] {'cols'}, use_global_device_ids=true, to_apply=%region_14.15 | all-reduce | flops 2048 | bytes 16384 | tf_op jit(solution)/shard_map/psum | solution.py:63
  625.4 0.1 dynamic_slice.40
  625.5 344.5 %all-reduce.2.cloned.1.call-done = f32[32,2048]{1,0:T(8,128)} async-done(((f32[32,2048]{1,0:T(8,128)}), f32[32,2048]{1,0:T(8,128)}) %all-reduce.2.cloned.1.call-update) | async-done | bytes 262160 | tf_op jit(solution)/shard_map/psum | solution.py:63
  970.0 1.4 dynamic-slice_divide_fusion
  (24 shorter events, 0.3 us)
Async XLA Ops:
  7.2 221.9 %copy-start.4 = (f32[512]{0:T(512)S(1)}, f32[512]{0:T(512)}, u32[]{:S(2)}) copy-start(f32[512]{0:T(512)} %param.7) | copy-start | bytes 6148
  7.2 962.8 %all-reduce.2.cloned.1.call-start = ((), (), s32[]{:S(2)}) async-start(), calls=%async_computation | async-start | bytes 524288 | tf_op jit(solution)/shard_map/psum | solution.py:63
  305.9 3.5 copy-start
  348.8 3.5 copy-start.1
  348.8 4.5 copy-start.3
  352.2 140.7 %copy-start.2 = (bf16[32,512]{1,0:T(8,128)(2,1)S(1)}, bf16[32,512]{1,0:T(8,128)(2,1)}, u32[]{:S(2)}) copy-start(bf16[32,512]{1,0:T(8,128)(2,1)} %param.6) | copy-start | bytes 98308
Sparse Core Ops, SparseCore 0:
  494.2 475.7 all-reduce.1

commit v2 on v0

--- a/solution.py
+++ b/solution.py
@@ -26,7 +26,10 @@
 
 def on_device(points, samples, potential):
     own_count = points.shape[1]
-    whole = lax.all_gather(points, "cols", axis=1, tiled=True)
+    size = lax.axis_size("cols")
+    tiles = jnp.stack([points for _ in range(size)])
+    tiles = lax.all_to_all(tiles, "cols", split_axis=0, concat_axis=0)
+    whole = jnp.concatenate(tiles, axis=1)
     block_count = whole.shape[1]
     col_count = lax.axis_size("cols")
     total_samples = samples.shape[1] * col_count

time: 1040 us -> 987 us (0.949)
  blocking collectives: 656 us -> 571 us
  starting transfers between devices: 0.04 us -> 19.7 us
  waiting for transfers between devices: 345 us -> 360 us
    all_gather x1 -> x0, blocking collectives: 86 us -> none  [on_device(): whole = lax.all_gather(points, 'cols', axis=1, tiled=True)]
    all_to_all x0 -> x1, starting transfers between devices: none -> 19.6 us  [on_device(): tiles = lax.all_to_all(tiles, 'cols', split_axis=0, concat_axis=0)]
    all_to_all x0 -> x1, waiting for transfers between devices: none -> 17.8 us  [on_device(): tiles = lax.all_to_all(tiles, 'cols', split_axis=0, concat_axis=0)]
  transfers between devices with their start and end apart: 1 -> 2, of which waited for: 1 -> 2; matrix products, arithmetic and copies ran while one was open for 0% -> 0% of each run, Pallas kernels for 0% -> 0%
where the time goes in v2:
time: 987 us
  blocking collectives  571 us (58%)
  waiting for transfers between devices  360 us (36%)
  starting transfers between devices  19.7 us (2%)
  between operations  14.2 us (1%)
  other arithmetic  13.3 us (1%)
    psum x1, waiting for transfers between devices, on_device(): numer_all, denom_all = lax.psum((numer_scaled, denom_scaled), 'cols')  342 us
    pmax x1, blocking collectives, on_device(): new_top = lax.pmax(block_top, 'cols')  140 us
    psum x1, blocking collectives, on_device(): lax.psum(jnp.sum(jnp.exp(score - row_top[:, None]), axis=1), 'cols')  131 us
    psum x1, blocking collectives, on_device(): numer_all, denom_all = lax.psum((numer_scaled, denom_scaled), 'cols')  131 us
    pmax x1, blocking collectives, on_device(): row_top = lax.pmax(jnp.max(score, axis=1), 'cols')  130 us
    all_gather x2, blocking collectives, joined(): gathered = jax.tree.map(lambda a: lax.all_gather(a, axis), part)  38.1 us
  transfers between devices with their start and end apart: 2, of which 2 were waited for; matrix products, arithmetic and copies ran while one was open for 0% of the time, Pallas kernels for 0%

profile of v2, /device:TPU:1, one launch (start us, length us, event | category | flops | bytes accessed | tf_op | source)
XLA Modules:
  0.0 986.8 jit_solution(2812798826475804950)
XLA Ops:
  7.2 0.0 copy-start.2
  7.2 0.0 copy-start.4
  7.2 0.8 stack.2
  8.0 1.1 reshape.52
  9.0 19.6 %all-to-all-start = ((bf16[64,2,512]{2,1,0:T(2,128)(2,1)}), bf16[64,2,512]{2,1,0:T(2,128)(2,1)S(1)}, u32[]{:S(2)}, u32[]{:S(2)}) async-start(bf16[64,2,512]{2,1,0:T(2,128)(2,1)} %reshape.52), calls=%async_computation | async-start | bytes 262144 | tf_op jit(solution)/shard_map/all_to_all | solution.py:31
  28.6 0.0 all-reduce.2.cloned.1.call-start
  28.7 0.8 multiply_reduce_fusion.1
  29.5 17.8 %all-to-all-done = bf16[64,2,512]{2,1,0:T(2,128)(2,1)S(1)} async-done(((bf16[64,2,512]{2,1,0:T(2,128)(2,1)}), bf16[64,2,512]{2,1,0:T(2,128)(2,1)S(1)}, u32[]{:S(2)}, u32[]{:S(2)}) %all-to-all-start) | async-done | bytes 131104 | tf_op jit(solution)/shard_map/all_to_all | solution.py:31
  47.2 0.3 reshape.53
  47.5 0.2 multiply_reduce_fusion
  47.8 0.1 mul.84
  47.8 0.2 copy.6
  48.0 0.5 reshape.37
  48.6 0.0 copy-done.2
  48.6 0.0 copy-done.4
  48.6 2.9 fusion
  51.5 130.5 %pmax.14 = f32[2048]{0:T(1024)S(1)} all-reduce(f32[2048]{0:T(1024)S(1)} %get-tuple-element.156), channel_id=1, replica_groups=mesh['rows'=8,'cols'=64] {'cols'}, use_global_device_ids=true, to_apply=%region_3.0 | all-reduce | flops 2048 | bytes 16384 | tf_op jit(solution)/shard_map/pmax | solution.py:46
  182.0 3.1 exponential_reduce_fusion.1
  185.1 131.3 %psum.21 = f32[2048]{0:T(1024)S(1)} all-reduce(f32[2048]{0:T(1024)S(1)} %exponential_reduce_fusion.1), channel_id=1, replica_groups=mesh['rows'=8,'cols'=64] {'cols'}, use_global_device_ids=true, to_apply=%region_5.0 | all-reduce | flops 2048 | bytes 16384 | tf_op jit(solution)/shard_map/psum | solution.py:47
  316.4 0.0 copy-start
  316.4 2.8 fusion.1
  319.2 0.6 copy-done
  319.8 0.9 exponential_reduce_fusion
  320.8 19.0 %all-gather.2 = f32[8,1,512]{2,1,0:T(1,128)S(1)} all-gather(f32[1,1,512]{2,1,0:T(1,128)S(1)} %bitcast.31), channel_id=2, replica_groups=mesh['rows'=8,'cols'=64] {'rows'}, dimensions={0}, use_global_device_ids=true | all-gather | bytes 18432 | tf_op jit(solution)/shard_map/all_gather | solution.py:11
  339.8 19.0 %all-gather.3 = f32[8,1,512]{2,1,0:T(1,128)S(1)} all-gather(f32[1,1,512]{2,1,0:T(1,128)S(1)} %bitcast.32), channel_id=3, replica_groups=mesh['rows'=8,'cols'=64] {'rows'}, dimensions={0}, use_global_device_ids=true | all-gather | bytes 18432 | tf_op jit(solution)/shard_map/all_gather | solution.py:11
  358.9 0.4 while.17
  359.3 0.0 copy-start.1
  359.3 0.0 copy-start.3
  359.3 2.8 fusion.2
  362.1 0.6 copy-done.1
  362.7 1.0 convert_reduce_fusion
  363.8 0.0 copy-done.3
  363.8 140.0 %pmax.15 = f32[2048]{0:T(1024)S(1)} all-reduce(f32[2048]{0:T(1024)S(1)} %fusion.2), channel_id=1, replica_groups=mesh['rows'=8,'cols'=64] {'cols'}, use_global_device_ids=true, to_apply=%region_11.12 | all-reduce | flops 2048 | bytes 16384 | tf_op jit(solution)/shard_map/pmax | solution.py:62
  503.8 1.2 fusion.3
  505.0 0.0 all-reduce.2.cloned.1.call-update
  505.0 0.6 dynamic_slice.36
  505.6 130.8 %psum.23 = f32[2048]{0:T(1024)S(1)} all-reduce(f32[2048]{0:T(1024)S(1)} %get-tuple-element.150), channel_id=1, replica_groups=mesh['rows'=8,'cols'=64] {'cols'}, use_global_device_ids=true, to_apply=%region_14.15 | all-reduce | flops 2048 | bytes 16384 | tf_op jit(solution)/shard_map/psum | solution.py:66
  636.4 0.1 dynamic_slice.40
  636.4 342.1 %all-reduce.2.cloned.1.call-done = f32[32,2048]{1,0:T(8,128)} async-done(((f32[32,2048]{1,0:T(8,128)}), f32[32,2048]{1,0:T(8,128)}) %all-reduce.2.cloned.1.call-update) | async-done | bytes 262160 | tf_op jit(solution)/shard_map/psum | solution.py:66
  978.6 1.4 dynamic-slice_divide_fusion
  (23 shorter events, 0.3 us)
Async XLA Ops:
  7.2 41.4 %copy-start.2 = (bf16[32,512]{1,0:T(8,128)(2,1)S(1)}, bf16[32,512]{1,0:T(8,128)(2,1)}, u32[]{:S(2)}) copy-start(bf16[32,512]{1,0:T(8,128)(2,1)} %param.6) | copy-start | bytes 98308
  7.2 41.4 %copy-start.4 = (f32[512]{0:T(512)S(1)}, f32[512]{0:T(512)}, u32[]{:S(2)}) copy-start(f32[512]{0:T(512)} %param.7) | copy-start | bytes 6148
  9.0 38.2 %all-to-all-start = ((bf16[64,2,512]{2,1,0:T(2,128)(2,1)}), bf16[64,2,512]{2,1,0:T(2,128)(2,1)S(1)}, u32[]{:S(2)}, u32[]{:S(2)}) async-start(bf16[64,2,512]{2,1,0:T(2,128)(2,1)} %reshape.52), calls=%async_computation | async-start | bytes 262144 | tf_op jit(solution)/shard_map/all_to_all | solution.py:31
  28.6 949.9 %all-reduce.2.cloned.1.call-start = ((), (), s32[]{:S(2)}) async-start(), calls=%async_computation.1 | async-start | bytes 524288 | tf_op jit(solution)/shard_map/psum | solution.py:66
  316.4 3.5 copy-start
  359.3 3.5 copy-start.1
  359.3 4.5 copy-start.3
Sparse Core Ops, SparseCore 0:
  505.1 473.4 all-reduce.1
